TPU v7x, 256 devices: a whole 4x4x8 slice. The times are simulated.
256 devices in a mesh: grp: 4 (over z_lo), dp: 8 (over y, z_hi), width: 8 (over x, core).
Axes of the slice: x: 4, y: 4, z: 8 (z_hi: 2, z_lo: 4; z = z_hi * 4 + z_lo), core: 2. Of those that a mesh axis runs over, the one named last changes fastest.
Arguments:
- query_out: bfloat16 [512, 8192], P(None, ('grp', 'dp')), may hold values from -0.125 to 0.125
- query_in: bfloat16 [512, 14336], P(None, 'width'), may hold values from -0.046875 to 0.046875
- eigen_out: bfloat16 [8192, 8192], P(('grp', 'dp'), 'width'), may hold values from -0.0625 to 0.0625
- eigen_in: bfloat16 [14336, 14336], P('width', ('grp', 'dp')), may hold values from -0.046875 to 0.046875
- eigvals: float32 [8192, 14336], P('width', ('grp', 'dp')), may hold values from 0.001 to 5
- start: bfloat16 [14336, 256], P(('grp', 'dp')), may hold values from -6 to 6
- grads_out: bfloat16 [16384, 8192], P(('grp', 'dp'), 'width'), may hold values from -0.0625 to 0.0625
- gate_pre: bfloat16 [16384, 14336], P(('grp', 'dp'), 'width'), may hold values from -6 to 6
- up_pre: bfloat16 [16384, 14336], P(('grp', 'dp'), 'width'), may hold values from -0.046875 to 0.046875
Outputs:
- scores: float32 [16, 16384], P(None, ('grp', 'dp', 'width'))
- out_factor: bfloat16 [8192, 256], P('width')
- in_factor: bfloat16 [14336, 256], P('width')
All inputs are finite; a program needn't handle non-finite values.
Results may differ from a plain program's by a relative error of at most 0.0095.
Values may be sent and summed in bfloat16 or wider, within the bound.
A program may use at most 128 MiB of HBM per device.

v0:
```python
import jax
import jax.numpy as jnp
from jax import lax
from jax.sharding import Mesh
from jax.sharding import PartitionSpec as P

D = 8192
NQ = 16
QTOK = 32
RANK = 16
ITERS = 2
GRP_DP = ("grp", "dp_0", "dp_1")
GRP_DP_WIDTH = ("grp", "dp_0", "dp_1", "width")


damping = 0.01
ridge_scale = 1e-06


def padded_to(lines, length):
    spare = -lines.shape[0] % length
    if not spare:
        return lines
    return jnp.concatenate([lines, jnp.zeros((spare, *lines.shape[1:]), lines.dtype)])


def total_of(array, axis):
    lines = array.reshape(-1, *array.shape[1:][-1:])
    padded = padded_to(lines, lax.axis_size(axis))
    own = lax.psum_scatter(padded, axis, scatter_dimension=0, tiled=True)
    whole = lax.all_gather(own, axis, axis=0, tiled=True)
    return whole[: len(lines)].reshape(array.shape)


def from_everyone(array, axis):
    length = lax.axis_size(axis)
    return lax.all_to_all(
        jnp.broadcast_to(array[None], (length, *array.shape)), axis, 0, 0, tiled=True
    )


def joined_along(blocks, dim):
    blocks = jnp.moveaxis(blocks, 0, dim)
    lengths = blocks.shape
    return blocks.reshape(*lengths[:dim], lengths[dim] * lengths[dim + 1], *lengths[dim + 2 :])


def gather_axes(array, axes, dim):
    far, near = axes
    leading = from_everyone(array, far)
    blocks = jnp.swapaxes(from_everyone(leading, near), 0, 1)
    return joined_along(blocks.reshape(-1, *array.shape), dim)


def in_blocks(array, dim, length):
    before, after = (array.shape[:dim], array.shape[dim + 1 :])
    return jnp.moveaxis(array.reshape(*before, length, -1, *after), dim, 0)


def sent_and_summed(array, axis, dim):
    blocks = in_blocks(array, dim, lax.axis_size(axis))
    arrived = lax.all_to_all(blocks, axis, split_axis=0, concat_axis=0, tiled=True)
    return arrived.sum(axis=0)


def sum_in_two_steps(array, axes, dim):
    far, near = axes
    blocks = in_blocks(array, dim, lax.axis_size(far))
    nearer = sent_and_summed(blocks, near, dim + 1)
    arrived = lax.all_to_all(nearer, far, split_axis=0, concat_axis=0, tiled=True)
    return arrived.sum(axis=0)


def total_of_2(array, axes):
    lines = array.reshape(-1, array.shape[-1])
    padded = padded_to(lines, lax.axis_size(axes[0]) * lax.axis_size(axes[1]))
    whole = gather_axes(sum_in_two_steps(padded, axes, 0), axes, 0)
    return lax.slice_in_dim(whole, 0, len(lines)).reshape(array.shape)


def collect(array, axis, dim):
    blocks = from_everyone(array, axis)
    return joined_along(blocks, dim)


def nested_sum(array, axes):
    lines = array.reshape(-1, array.shape[-1])
    padded = padded_to(lines, lax.axis_size(axes))
    whole = collect(sent_and_summed(padded, axes, 0), axes, 0)
    return lax.slice_in_dim(whole, 0, len(lines)).reshape(array.shape)


def over_copies(array, axis):
    return from_everyone(array, axis).sum(axis=0)


def in_one_piece(arrays, axis, dim, along):
    both = jnp.concatenate(arrays, axis=along)
    whole, at, outs = (lax.psum_scatter(both, axis, scatter_dimension=dim, tiled=True), 0, [])
    for a in arrays:
        outs.append(lax.slice_in_dim(whole, at, at + a.shape[along], axis=along))
        at += a.shape[along]
    return tuple(outs)


def local_gram(image_cols):
    return jnp.einsum("dqr,dqs->qrs", image_cols, image_cols, precision=lax.Precision.HIGHEST) / D


def factor_inverse(gram_mat, identity):
    trace_mean = jnp.trace(gram_mat, axis1=1, axis2=2) / RANK
    gram_mat = gram_mat + ridge_scale * trace_mean[:, None, None] * identity[None, :, :]
    lower_factor = jnp.linalg.cholesky(gram_mat)

    def invert_one(single_lower):
        return jax.scipy.linalg.solve_triangular(single_lower, identity, lower=True)

    return jax.vmap(invert_one)(lower_factor)


def per_device(
    query_out, query_in, eigen_out, eigen_in, eigvals, start, grads_out, gate_pre, up_pre
):
    part_out = jnp.dot(query_out, eigen_out, preferred_element_type=jnp.float32)
    part_in = jnp.dot(query_in, eigen_in, preferred_element_type=jnp.float32)
    rot_in = total_of(part_in, "width").astype(jnp.bfloat16)
    rot_out = total_of_2(part_out, ("grp", ("dp_0", "dp_1"))).astype(jnp.bfloat16)
    rows_out = rot_out.shape[1]
    cols_in = rot_in.shape[1]
    rotated = jnp.einsum(
        "qkd,qkf->qdf",
        rot_out.reshape(NQ, QTOK, rows_out),
        rot_in.reshape(NQ, QTOK, cols_in),
        preferred_element_type=jnp.float32,
    )
    rotated = (rotated / (eigvals + damping)).astype(jnp.bfloat16)
    basis_in = start.reshape(cols_in, NQ, RANK)
    identity = jnp.eye(RANK, dtype=jnp.float32)
    basis_out = None
    for iteration in range(ITERS):
        image_cols = jnp.einsum(
            "qdf,fqr->dqr", rotated, basis_in, preferred_element_type=jnp.float32
        )
        image_cols = nested_sum(image_cols, GRP_DP)
        gram_mat = over_copies(local_gram(image_cols), "width")
        inverse = factor_inverse(gram_mat, identity)
        basis_out = jnp.einsum(
            "dqr,qsr->dqs", image_cols, inverse, precision=lax.Precision.HIGHEST
        ).astype(jnp.bfloat16)
        returned = jnp.einsum(
            "qdf,dqr->fqr", rotated, basis_out, preferred_element_type=jnp.float32
        )
        basis_in = over_copies(returned, "width").astype(jnp.bfloat16)
    out_cols = basis_out.reshape(rows_out, NQ * RANK)
    in_cols = basis_in.reshape(cols_in, NQ * RANK)
    part_factor_in = jnp.dot(eigen_in, in_cols, preferred_element_type=jnp.float32)
    part_factor_out = jnp.dot(eigen_out, out_cols, preferred_element_type=jnp.float32)
    in_factor = total_of_2(part_factor_in, ("grp", ("dp_0", "dp_1"))).astype(jnp.bfloat16)
    block_factor = over_copies(part_factor_out, "width").astype(jnp.bfloat16)
    whole_out = lax.all_gather(block_factor, GRP_DP, axis=0, tiled=True)
    width_rows = grads_out.shape[1]
    out_factor = lax.dynamic_slice_in_dim(
        whole_out, lax.axis_index("width") * width_rows, width_rows, 0
    )
    hidden = (jax.nn.silu(gate_pre.astype(jnp.float32)) * up_pre.astype(jnp.float32)).astype(
        jnp.bfloat16
    )
    proj_out = jnp.dot(grads_out, out_factor, preferred_element_type=jnp.float32)
    proj_in = jnp.dot(hidden, in_factor, preferred_element_type=jnp.float32)
    proj_out, proj_in = in_one_piece((proj_out, proj_in), "width", 0, 1)
    scores = (proj_out * proj_in).reshape(proj_out.shape[0], NQ, RANK).sum(axis=2).T
    return (scores, out_factor, in_factor)


def solution(mesh):
    finer = Mesh(
        mesh.devices.reshape(mesh.shape["grp"], 4, 2, mesh.shape["width"]),
        ("grp", "dp_0", "dp_1", "width"),
    )
    placed = (
        P(None, GRP_DP),
        P(None, "width"),
        P(GRP_DP, "width"),
        P("width", GRP_DP),
        P("width", GRP_DP),
        P(GRP_DP, None),
        P(GRP_DP, "width"),
        P(GRP_DP, "width"),
        P(GRP_DP, "width"),
    )
    return jax.shard_map(
        per_device,
        mesh=finer,
        in_specs=placed,
        out_specs=(P(None, GRP_DP_WIDTH), P("width", None), P("width", None)),
        check_vma=False,
    )
```

profile of v0, /device:TPU:1, one launch (start us, length us, event | category | flops | bytes accessed | tf_op | source)
XLA Modules:
  0.0 939.0 jit_solution(1669445982877719687)
XLA Ops:
  9.1 47.6 %all_to_all.85 = f32[8,4,16,1024]{3,2,1,0:T(8,128)} all-to-all(f32[8,4,16,1024]{3,2,1,0:T(8,128)S(1)} %bitcast.96), channel_id=1, replica_groups=mesh['grp'=4,'dp_0'=4,'dp_1'=2,'width'=8] {'dp_0','dp_1'}, dimensions={0} | all-to-all | bytes 4194304 | tf_op jit(solution)/shard_map/all_to_all | solution.py:62
  59.2 19.1 %all-to-all-start.1 = ((f32[4,16,1024]{2,1,0:T(8,128)}), f32[4,16,1024]{2,1,0:T(8,128)}, u32[]{:S(2)}, u32[]{:S(2)}) async-start(f32[4,16,1024]{2,1,0:T(8,128)} %reduce_sum.124), calls=%async_computation.1 | async-start | bytes 524288 | tf_op jit(solution)/shard_map/all_to_all | solution.py:70
  86.2 8.6 all_to_all.86
  101.2 12.2 %reduce-scatter.5.cloned.1.call-done = f32[64,448]{1,0:T(8,128)} async-done(((f32[512,448]{1,0:T(8,128)}), f32[64,448]{1,0:T(8,128)}) %reduce-scatter.5.cloned.1.call-update) | async-done | bytes 114704 | tf_op jit(solution)/shard_map/reduce_scatter | solution.py:30
  113.4 16.7 %all_gather.6 = f32[512,448]{1,0:T(8,128)S(1)} all-gather(f32[64,448]{1,0:T(8,128)} %reduce-scatter.5.cloned.1.call-done), channel_id=1, replica_groups=mesh['grp'=4,'dp_0'=4,'dp_1'=2,'width'=8] {'width'}, dimensions={0}, use_global_device_ids=true | all-gather | bytes 1032192 | tf_op jit(solution)/shard_map/all_gather | solution.py:31
  130.3 5.5 divide_convert_fusion
  147.7 7.6 reshape_reshape.21
  155.9 34.5 %all_to_all.87 = f32[32,512,16]{1,2,0:T(8,128)S(1)} all-to-all(f32[32,512,16]{1,2,0:T(8,128)S(1)} %copy.89), channel_id=1, replica_groups=mesh['grp'=4,'dp_0'=4,'dp_1'=2,'width'=8] {'grp','dp_0','dp_1'}, dimensions={0} | all-to-all | bytes 2097152 | tf_op jit(solution)/shard_map/all_to_all | solution.py:62
  191.6 8.6 all-to-all-start.5
  200.3 25.0 %all-to-all-done.5 = f32[32,512,16]{1,2,0:T(8,128)S(1)} async-done(((f32[32,512,16]{1,2,0:T(8,128)}), f32[32,512,16]{1,2,0:T(8,128)S(1)}, u32[]{:S(2)}, u32[]{:S(2)}) %all-to-all-start.5) | async-done | bytes 1048608 | tf_op jit(solution)/shard_map/all_to_all | solution.py:37
  238.4 7.1 all-to-all-start.6
  253.3 23.5 %custom-call.8 = f32[16,16,16]{2,1,0:T(8,128)S(1)} custom-call(f32[16,16,16]{2,1,0:T(8,128)S(1)} %fusion.15), custom_call_target="Cholesky" | custom-call | tf_op jit(solution)/shard_map/jit(cholesky)/cholesky | solution.py:113
  277.0 19.8 %custom-call.9 = f32[16,1,16,16]{2,3,1,0:T(8,128)S(1)} custom-call(f32[16,1,16,16]{3,2,1,0:T(8,128)S(1)} %select_bitcast_fusion.1), custom_call_target="InvertDiagBlocksLowerTriangular" | custom-call | tf_op jit(solution)/shard_map/vmap(jit(_solve_triangular))/triangular_solve | solution.py:116
  298.3 9.1 convolution_bitcast_fusion.5
  307.9 53.0 %all_to_all.88 = f32[8,448,16,16]{1,3,2,0:T(8,128)} all-to-all(f32[8,448,16,16]{1,3,2,0:T(8,128)S(1)} %broadcast_in_dim.48), channel_id=1, replica_groups=mesh['grp'=4,'dp_0'=4,'dp_1'=2,'width'=8] {'width'}, dimensions={0} | all-to-all | bytes 7340032 | tf_op jit(solution)/shard_map/all_to_all | solution.py:37
  363.6 7.2 convolution_bitcast_fusion.2
  375.5 7.6 reshape_reshape.23
  383.7 30.4 %all_to_all.89 = f32[32,512,16]{1,2,0:T(8,128)S(1)} all-to-all(f32[32,512,16]{1,2,0:T(8,128)S(1)} %copy.100), channel_id=1, replica_groups=mesh['grp'=4,'dp_0'=4,'dp_1'=2,'width'=8] {'grp','dp_0','dp_1'}, dimensions={0} | all-to-all | bytes 2097152 | tf_op jit(solution)/shard_map/all_to_all | solution.py:62
  414.3 32.3 %all_to_all.90 = f32[32,512,16]{1,2,0:T(8,128)S(1)} all-to-all(f32[32,512,16]{1,2,0:T(8,128)S(1)} %broadcast_in_dim.49), channel_id=1, replica_groups=mesh['grp'=4,'dp_0'=4,'dp_1'=2,'width'=8] {'grp','dp_0','dp_1'}, dimensions={0} | all-to-all | bytes 2097152 | tf_op jit(solution)/shard_map/all_to_all | solution.py:37
  459.2 12.1 %all_to_all.91 = f32[8,1,4096]{2,1,0:T(1,128)S(1)} all-to-all(f32[8,1,4096]{2,1,0:T(1,128)S(1)} %reshape.70), channel_id=1, replica_groups=mesh['grp'=4,'dp_0'=4,'dp_1'=2,'width'=8] {'width'}, dimensions={0} | all-to-all | bytes 262144 | tf_op jit(solution)/shard_map/all_to_all | solution.py:37
  473.3 23.5 %custom-call.10 = f32[16,16,16]{2,1,0:T(8,128)S(1)} custom-call(f32[16,16,16]{2,1,0:T(8,128)S(1)} %fusion.12), custom_call_target="Cholesky" | custom-call | tf_op jit(solution)/shard_map/jit(cholesky)/cholesky | solution.py:113
  497.0 19.8 %custom-call.11 = f32[16,1,16,16]{2,3,1,0:T(8,128)S(1)} custom-call(f32[16,1,16,16]{3,2,1,0:T(8,128)S(1)} %select_bitcast_fusion), custom_call_target="InvertDiagBlocksLowerTriangular" | custom-call | tf_op jit(solution)/shard_map/vmap(jit(_solve_triangular))/triangular_solve | solution.py:116
  525.4 9.1 convolution_bitcast_fusion.4
  534.5 17.3 %all-to-all-done.11 = f32[8,256,256]{2,1,0:T(8,128)} async-done(((f32[8,256,256]{2,1,0:T(8,128)}), f32[8,256,256]{2,1,0:T(8,128)}, u32[]{:S(2)}, u32[]{:S(2)}) %all-to-all-start.11) | async-done | bytes 2097184 | tf_op jit(solution)/shard_map/all_to_all | solution.py:37
  562.2 46.2 %all-to-all-done.12 = f32[8,448,16,16]{1,3,2,0:T(8,128)} async-done(((f32[8,448,16,16]{1,3,2,0:T(8,128)}), f32[8,448,16,16]{1,3,2,0:T(8,128)}, u32[]{:S(2)}, u32[]{:S(2)}) %all-to-all-start.12) | async-done | bytes 3670048 | tf_op jit(solution)/shard_map/all_to_all | solution.py:37
  616.9 69.4 %all_to_all.92 = f32[8,4,56,256]{3,2,1,0:T(8,128)} all-to-all(f32[8,4,56,256]{3,2,1,0:T(8,128)S(1)} %copy.111), channel_id=1, replica_groups=mesh['grp'=4,'dp_0'=4,'dp_1'=2,'width'=8] {'dp_0','dp_1'}, dimensions={0} | all-to-all | bytes 3670016 | tf_op jit(solution)/shard_map/all_to_all | solution.py:62
  688.0 8.5 all_to_all.93
  696.5 18.5 %all_to_all.94 = bf16[4,56,256]{2,1,0:T(8,128)(2,1)S(1)} all-to-all(bf16[4,56,256]{2,1,0:T(8,128)(2,1)S(1)} %broadcast_in_dim.53), channel_id=1, replica_groups=mesh['grp'=4,'dp_0'=4,'dp_1'=2,'width'=8] {'grp'}, dimensions={0} | all-to-all | bytes 229376 | tf_op jit(solution)/shard_map/all_to_all | solution.py:37
  716.0 11.7 %all-to-all-start.16 = ((bf16[8,4,56,256]{3,2,1,0:T(8,128)(2,1)}), bf16[8,4,56,256]{3,2,1,0:T(8,128)(2,1)S(1)}, u32[]{:S(2)}, u32[]{:S(2)}) async-start(bf16[8,4,56,256]{3,2,1,0:T(8,128)(2,1)} %broadcast_in_dim.54), calls=%async_computation.17 | async-start | bytes 1835008 | tf_op jit(solution)/shard_map/all_to_all | solution.py:37
  727.8 23.5 %all-to-all-done.16 = bf16[8,4,56,256]{3,2,1,0:T(8,128)(2,1)S(1)} async-done(((bf16[8,4,56,256]{3,2,1,0:T(8,128)(2,1)}), bf16[8,4,56,256]{3,2,1,0:T(8,128)(2,1)S(1)}, u32[]{:S(2)}, u32[]{:S(2)}) %all-to-all-start.16) | async-done | bytes 917536 | tf_op jit(solution)/shard_map/all_to_all | solution.py:37
  756.1 114.8 %all-gather.2.cloned.1.call-done = bf16[8192,256]{1,0:T(8,128)(2,1)} async-done(((bf16[256,256]{1,0:T(8,128)(2,1)}), bf16[8192,256]{1,0:T(8,128)(2,1)}) %all-gather.2.cloned.1.call-update) | async-done | bytes 4194320 | tf_op jit(solution)/shard_map/all_gather | solution.py:160
  875.1 55.4 %reduce-scatter.7.cloned.1.call-done = f32[64,512]{1,0:T(8,128)} async-done(((f32[512,512]{1,0:T(8,128)}), f32[64,512]{1,0:T(8,128)}) %reduce-scatter.7.cloned.1.call-update) | async-done | bytes 131088
  (125 shorter events, 119.4 us)
Async XLA Ops:
  7.2 71.1 %copy-start = (bf16[512,1792]{1,0:T(8,128)(2,1)S(1)}, bf16[512,1792]{1,0:T(8,128)(2,1)}, u32[]{:S(2)}) copy-start(bf16[512,1792]{1,0:T(8,128)(2,1)} %param.13) | copy-start | bytes 5505028
  9.1 69.2 %copy-start.6 = (bf16[1792,448]{0,1:T(8,128)(2,1)S(1)}, bf16[1792,448]{0,1:T(8,128)(2,1)}, u32[]{:S(2)}) copy-start(bf16[1792,448]{0,1:T(8,128)(2,1)} %param.15) | copy-start | bytes 4816900
  59.2 26.0 %all-to-all-start.1 = ((f32[4,16,1024]{2,1,0:T(8,128)}), f32[4,16,1024]{2,1,0:T(8,128)}, u32[]{:S(2)}, u32[]{:S(2)}) async-start(f32[4,16,1024]{2,1,0:T(8,128)} %reduce_sum.124), calls=%async_computation.1 | async-start | bytes 524288 | tf_op jit(solution)/shard_map/all_to_all | solution.py:70
  78.3 35.1 %reduce-scatter.5.cloned.1.call-start = ((), (), s32[]{:S(2)}) async-start(), calls=%async_computation.19 | async-start | bytes 1179648 | tf_op jit(solution)/shard_map/reduce_scatter | solution.py:30
  80.4 19.1 %copy-start.10 = (bf16[448,256]{1,0:T(8,128)(2,1)S(1)}, bf16[448,256]{1,0:T(8,128)(2,1)}, u32[]{:S(2)}) copy-start(bf16[448,256]{1,0:T(8,128)(2,1)} %param.17) | copy-start | bytes 688132
  80.4 19.2 %copy-start.5 = (f32[1024,448]{0,1:T(8,128)S(1)}, f32[1024,448]{0,1:T(8,128)}, u32[]{:S(2)}) copy-start(f32[1024,448]{0,1:T(8,128)} %param.16) | copy-start | bytes 5505028
  95.9 34.3 %all-to-all-start.3 = ((bf16[8,4,16,1024]{3,2,1,0:T(8,128)(2,1)}), bf16[8,4,16,1024]{3,2,1,0:T(8,128)(2,1)S(1)}, u32[]{:S(2)}, u32[]{:S(2)}) async-start(bf16[8,4,16,1024]{3,2,1,0:T(8,128)(2,1)} %broadcast_in_dim.43), calls=%async_computation.3 | async-start | bytes 2097152 | tf_op jit(solution)/shard_map/all_to_all | solution.py:37
  135.7 5.2 copy-start.2
  191.6 33.6 %all-to-all-start.5 = ((f32[32,512,16]{1,2,0:T(8,128)}), f32[32,512,16]{1,2,0:T(8,128)S(1)}, u32[]{:S(2)}, u32[]{:S(2)}) async-start(f32[32,512,16]{1,2,0:T(8,128)} %broadcast_in_dim.44), calls=%async_computation.6 | async-start | bytes 2097152 | tf_op jit(solution)/shard_map/all_to_all | solution.py:37
  238.4 12.3 %all-to-all-start.6 = ((f32[8,1,4096]{2,1,0:T(1,128)}), f32[8,1,4096]{2,1,0:T(1,128)S(1)}, u32[]{:S(2)}, u32[]{:S(2)}) async-start(f32[8,1,4096]{2,1,0:T(1,128)} %reshape.68), calls=%async_computation.7 | async-start | bytes 262144 | tf_op jit(solution)/shard_map/all_to_all | solution.py:37
  458.8 59.5 %copy-start.3 = (bf16[256,1024]{1,0:T(8,128)(2,1)S(1)}, bf16[256,1024]{1,0:T(8,128)(2,1)}, u32[]{:S(2)}) copy-start(bf16[256,1024]{1,0:T(8,128)(2,1)} %param.14) | copy-start | bytes 1572868
  520.3 31.4 %all-to-all-start.11 = ((f32[8,256,256]{2,1,0:T(8,128)}), f32[8,256,256]{2,1,0:T(8,128)}, u32[]{:S(2)}, u32[]{:S(2)}) async-start(f32[8,256,256]{2,1,0:T(8,128)} %broadcast_in_dim.51), calls=%async_computation.12 | async-start | bytes 4194304 | tf_op jit(solution)/shard_map/all_to_all | solution.py:37
  554.3 54.2 %all-to-all-start.12 = ((f32[8,448,16,16]{1,3,2,0:T(8,128)}), f32[8,448,16,16]{1,3,2,0:T(8,128)}, u32[]{:S(2)}, u32[]{:S(2)}) async-start(f32[8,448,16,16]{1,3,2,0:T(8,128)} %broadcast_in_dim.52), calls=%async_computation.13 | async-start | bytes 8388608 | tf_op jit(solution)/shard_map/all_to_all | solution.py:37
  559.6 52.3 %copy-start.7 = (bf16[1792,448]{0,1:T(8,128)(2,1)S(1)}, bf16[1792,448]{0,1:T(8,128)(2,1)}, u32[]{:S(2)}) copy-start(bf16[1792,448]{0,1:T(8,128)(2,1)} %param.15) | copy-start | bytes 4816900
  559.7 311.2 %all-gather.2.cloned.1.call-start = ((), (), s32[]{:S(2)}) async-start(), calls=%async_computation.20 | async-start | bytes 4325376 | tf_op jit(solution)/shard_map/all_gather | solution.py:160
  716.0 35.3 %all-to-all-start.16 = ((bf16[8,4,56,256]{3,2,1,0:T(8,128)(2,1)}), bf16[8,4,56,256]{3,2,1,0:T(8,128)(2,1)S(1)}, u32[]{:S(2)}, u32[]{:S(2)}) async-start(bf16[8,4,56,256]{3,2,1,0:T(8,128)(2,1)} %broadcast_in_dim.54), calls=%async_computation.17 | async-start | bytes 1835008 | tf_op jit(solution)/shard_map/all_to_all | solution.py:37
  727.7 202.8 %reduce-scatter.7.cloned.1.call-start = ((), (), s32[]{:S(2)}) async-start(), calls=%async_computation.21 | async-start | bytes 1179648
  751.4 4.7 copy-start.9
  751.4 120.7 %copy-start.8 = (bf16[512,1024]{1,0:T(8,128)(2,1)S(1)}, bf16[512,1024]{1,0:T(8,128)(2,1)}, u32[]{:S(2)}) copy-start(bf16[512,1024]{1,0:T(8,128)(2,1)} %param.18) | copy-start | bytes 3145732
  870.9 61.3 %copy-start.1 = (bf16[512,1792]{1,0:T(8,128)(2,1)S(1)}, bf16[512,1792]{1,0:T(8,128)(2,1)}, u32[]{:S(2)}) copy-start(bf16[512,1792]{1,0:T(8,128)(2,1)} %param.13) | copy-start | bytes 5505028
  872.1 3.0 copy-start.4
Sparse Core Ops, SparseCore 0:
  81.6 31.7 reduce-scatter.4
  562.3 308.5 all-gather.1
  875.2 55.2 reduce-scatter.6
where the time goes:
time: 950 us; the launch traced here: 939 us
  blocking collectives  332 us (35%)
  waiting for transfers between devices  304 us (32%)
  other arithmetic  107 us (11%)
  local copies, waits for them, and re-layouts  71.4 us (8%)
  starting transfers between devices  60.7 us (6%)
  matrix products  49.3 us (5%)
  between operations  14.5 us (2%)
    all_to_all x4, blocking collectives, sent_and_summed(): lax.all_to_all(blocks, axis, split_axis=0, concat_axis=0, tiled=True)  182 us
    all_to_all x5, blocking collectives, from_everyone(): lax.all_to_all(jnp.broadcast_to(array[None], (length, *array.shape)), axi...  125 us
    all_to_all x6, waiting for transfers between devices, from_everyone(): lax.all_to_all(jnp.broadcast_to(array[None], (length, *array.shape)), axi...  117 us
    all_gather x1, waiting for transfers between devices, per_device(): whole_out = lax.all_gather(block_factor, GRP_DP, axis=0, tiled=True)  115 us
    unnamed x4, waiting for transfers between devices  55.4 us
    another operation x6, other arithmetic, factor_inverse(): lower_factor = jnp.linalg.cholesky(gram_mat)  47.1 us
    all_to_all x6, starting transfers between devices, from_everyone(): lax.all_to_all(jnp.broadcast_to(array[None], (length, *array.shape)), axi...  41.5 us
    another operation x5, other arithmetic, invert_one(): return jax.scipy.linalg.solve_triangular(single_lower, identity, lower=True)  39.8 us
  transfers between devices with their start and end apart: 10, of which 9 were waited for; matrix products, arithmetic and copies ran while one was open for 4% of the time, Pallas kernels for 0%

commit v1 on v0

v1 whole, which is shorter than its diff:
```python
import jax
import jax.numpy as jnp
from jax import lax
from jax.experimental import pallas as pl
from jax.experimental.pallas import tpu as pltpu
from jax.sharding import Mesh
from jax.sharding import PartitionSpec as P

D = 8192
NQ = 16
QTOK = 32
RANK = 16
ITERS = 2
NY = 4
NZ = 8
NW = 8
QR = NQ * RANK
KQ = NQ * QTOK
damping = 0.01
ridge_scale = 1e-06

GRP_DP = ("grp", "dp_0", "dp_1")
GRP_DP_WIDTH = ("grp", "dp_0", "dp_1", "width")
MESH = pl.DeviceIdType.MESH
BF = jnp.bfloat16
F32 = jnp.float32
HIGHEST = lax.Precision.HIGHEST

Y_ORDER = (2, 1, 3)
Z_ORDER = (4, 3, 5, 2, 6, 1, 7)
W_ORDER = (4, 5, 3, 2, 6, 7, 1)
N_SEMS = 320

NN = (((1,), (0,)), ((), ()))
NT = (((1,), (1,)), ((), ()))
TN = (((0,), (0,)), ((), ()))


def mm(a, b, dims, precision=None):
    return lax.dot_general(a, b, dims, precision=precision, preferred_element_type=F32)


def rows_at(start, size):
    return pl.ds(pl.multiple_of(start, size), size)


def inverse_of_factor(gram):
    row = lax.broadcasted_iota(jnp.int32, (RANK, RANK), 0)
    col = lax.broadcasted_iota(jnp.int32, (RANK, RANK), 1)
    eye = (row == col).astype(F32)
    trace_mean = jnp.sum(gram * eye, keepdims=True) / RANK
    left = gram + ridge_scale * trace_mean * eye
    right = eye
    for k in range(RANK):
        scale = 1.0 / jnp.sqrt(left[k : k + 1, k : k + 1])
        row_left = left[k : k + 1, :] * scale
        row_right = right[k : k + 1, :] * scale
        column = jnp.where(row[:, :1] > k, left[:, k : k + 1] * scale, 0.0)
        left = left - column * row_left
        right = jnp.where(row == k, row_right, right - column * row_right)
    return right


def layout_of(shapes):
    rows = shapes["eo"][0]
    width_rows = shapes["eo"][1]
    ff_w, ff_r = shapes["ei"]
    tokens = shapes["go"][0]
    fp = -(-ff_r // 128) * 128
    scratch = dict(
        qo=(shapes["qo"], BF),
        qi=(shapes["qi"], BF),
        eo=(shapes["eo"], BF),
        ei=(shapes["ei"], BF),
        ev=(shapes["ev"], F32),
        st=(shapes["st"], BF),
        go=(shapes["go"], BF),
        ga=(shapes["ga"], BF),
        up=(shapes["up"], BF),
        hid=(shapes["ga"], BF),
        inv=((width_rows, fp), F32),
        rot=((NQ, width_rows, fp), BF),
        ro_send=((KQ, width_rows), BF),
        ro_recv=((NY - 1, KQ // NY, width_rows), BF),
        ro_z=((KQ // NY, width_rows), BF),
        ro_zrecv=((NZ - 1, KQ // 32, width_rows), BF),
        ro=((KQ, width_rows), BF),
        ri_send=((KQ, fp), BF),
        ri_recv=((NW - 1, KQ // NW, fp), BF),
        ri=((KQ, fp), BF),
        bi0=((QR, fp), BF),
    )
    for it in range(ITERS):
        scratch |= {
            f"im_send{it}": ((QR, width_rows), BF),
            f"im_recv{it}": ((NY - 1, QR // NY, width_rows), BF),
            f"im_z{it}": ((QR // NY, width_rows), BF),
            f"im_zrecv{it}": ((NZ - 1, RANK, width_rows // 2), BF),
            f"gram{it}": ((2 * NW, RANK, RANK), F32),
            f"bo{it}": ((QR, width_rows), BF),
            f"re_send{it}": ((QR, fp), BF),
            f"re_recv{it}": ((NW - 1, QR // NW, fp), BF),
            f"bi{it + 1}": ((QR, fp), BF),
        }
    scratch |= dict(
        of_send=((rows, QR), BF),
        of_recv=((NW - 1, rows // NW, QR), BF),
        of_part=((rows // NW, QR), BF),
        of_block=((rows, QR), BF),
        of=((width_rows, QR), BF),
        if_send=((ff_w, QR), BF),
        if_recv=((NY - 1, ff_w // NY, QR), BF),
        if_z=((ff_w // NY, QR), BF),
        if_zrecv=((NZ - 1, ff_w // 16, QR // 2), BF),
        inf=((ff_w, QR), BF),
        po_send=((tokens, QR), BF),
        po_recv=((NW - 1, tokens // NW, QR), BF),
        pi_send=((tokens, QR), BF),
        pi_recv=((NW - 1, tokens // NW, QR), BF),
        sc=((NQ, tokens // NW), F32),
    )
    return scratch


INPUTS = ("qo", "qi", "eo", "ei", "ev", "st", "go", "ga", "up")
OUTPUTS = ("sc", "of", "inf")


def make_kernel(names):
    def kernel(*refs):
        hbm = dict(zip(INPUTS, refs))
        out = dict(zip(OUTPUTS, refs[len(INPUTS) :]))
        r = dict(zip(names, refs[len(INPUTS) + len(OUTPUTS) :]))
        send_sem, recv_sem, in_sem, out_sem = refs[-4:]

        zlo, y, zhi, w = (lax.axis_index(name) for name in GRP_DP_WIDTH)
        z = zhi * 4 + zlo
        width_rows = r["eo"].shape[1]
        ff_w, ff_r = r["ei"].shape
        fp = r["inv"].shape[1]
        tokens = r["go"].shape[0]

        def y_at(dy):
            return lax.rem(y + dy, NY)

        def z_at(dz):
            return lax.rem(z + dz, NZ)

        def w_at(dw):
            return lax.rem(w + dw, NW)

        def y_dev(dy):
            return (zlo, y_at(dy), zhi, w)

        def z_dev(dz):
            zz = z_at(dz)
            return (lax.rem(zz, 4), y, zz // 4, w)

        def w_dev(dw):
            return (zlo, y, zhi, w_at(dw))

        def pair_dev(dw):
            return (zlo + 1 - 2 * lax.rem(zlo, 2), y, zhi, w_at(dw))

        loads = {}
        for i, name in enumerate(("qo", "eo", "qi", "ei", "ev", "st", "ga", "up", "go")):
            loads[name] = pltpu.make_async_copy(hbm[name], r[name], in_sem.at[i])
            loads[name].start()

        barrier = pltpu.get_barrier_semaphore()
        partners = [y_dev(d) for d in Y_ORDER] + [z_dev(d) for d in Z_ORDER]
        partners += [w_dev(d) for d in W_ORDER] + [pair_dev(d) for d in range(1, NW)]
        for partner in partners:
            pl.semaphore_signal(barrier, inc=1, device_id=partner, device_id_type=MESH)

        count = [0]
        unsent = []

        def copy_to(src, dst, device):
            k = count[0]
            count[0] += 1
            return pltpu.make_async_remote_copy(
                src_ref=src,
                dst_ref=dst,
                send_sem=send_sem.at[k],
                recv_sem=recv_sem.at[k],
                device_id=device,
                device_id_type=MESH,
            )

        def send(src, dst, device):
            copy = copy_to(src, dst, device)
            copy.start()
            unsent.append(copy)
            return copy

        def arrive(copies):
            for copy in copies:
                copy.wait_recv()

        def sum_into(dst, own, own_at, recv, n, step):
            total = dst.shape[0]

            def body(i, carry):
                at = rows_at(i * step, step)
                acc = own[rows_at(own_at + i * step, step), :].astype(F32)
                for s in range(n):
                    acc = acc + recv[s, at, :].astype(F32)
                dst[at, :] = acc.astype(dst.dtype)
                return carry

            lax.fori_loop(0, total // step, body, 0)

        loads["qo"].wait()
        loads["eo"].wait()
        yrows = KQ // NY
        ro_y = []
        for dy in Y_ORDER + (0,):
            at = rows_at(y_at(dy) * yrows, yrows)
            part = mm(r["qo"][at, :], r["eo"][...], NN)
            r["ro_send"][at, :] = part.astype(BF)
            if dy == Y_ORDER[0]:
                pl.semaphore_wait(barrier, len(partners))
            if dy:
                ro_y.append(send(r["ro_send"].at[at, :], r["ro_recv"].at[dy - 1], y_dev(dy)))

        loads["qi"].wait()
        loads["ei"].wait()
        wrows = KQ // NW
        r["ri_send"][...] = jnp.zeros((KQ, fp), BF)

        def part_in(i, carry):
            at = rows_at(i * 128, 128)
            r["ri_send"][at, :ff_r] = mm(r["qi"][at, :], r["ei"][...], NN).astype(BF)
            return carry

        lax.fori_loop(0, KQ // 128, part_in, 0)
        ri_w = []
        for dw in W_ORDER:
            at = rows_at(w_at(dw) * wrows, wrows)
            ri_w.append(send(r["ri_send"].at[at, :], r["ri_recv"].at[dw - 1], w_dev(dw)))

        loads["ev"].wait()
        r["inv"][...] = jnp.zeros((width_rows, fp), F32)

        def invert(i, carry):
            at = rows_at(i * 64, 64)
            r["inv"][at, :ff_r] = 1.0 / (r["ev"][at, :] + damping)
            return carry

        lax.fori_loop(0, width_rows // 64, invert, 0)

        arrive(ro_y)
        sum_into(r["ro_z"], r["ro_send"], y * yrows, r["ro_recv"], NY - 1, 16)
        zrows = yrows // NZ
        ro_z = []
        for dz in Z_ORDER:
            at = rows_at(z_at(dz) * zrows, zrows)
            ro_z.append(send(r["ro_z"].at[at, :], r["ro_zrecv"].at[dz - 1], z_dev(dz)))

        arrive(ri_w)
        own_in = rows_at(w * wrows, wrows)
        sum_into(r["ri"].at[own_in, :], r["ri_send"], w * wrows, r["ri_recv"], NW - 1, 16)
        ri_g = [send(r["ri"].at[own_in, :], r["ri"].at[own_in, :], w_dev(dw)) for dw in W_ORDER]

        loads["st"].wait()
        r["bi0"][...] = jnp.zeros((QR, fp), BF)
        r["bi0"][:, :ff_r] = r["st"][...].astype(F32).T.astype(BF)

        arrive(ro_z)
        own_out = rows_at(y * yrows + z * zrows, zrows)
        sum_into(r["ro"].at[own_out, :], r["ro_z"], z * zrows, r["ro_zrecv"], NZ - 1, 16)
        ro_g = [send(r["ro"].at[own_out, :], r["ro"].at[own_out, :], z_dev(dz)) for dz in Z_ORDER]

        loads["ga"].wait()
        loads["up"].wait()

        def hide(i, carry):
            at = rows_at(i * 16, 16)
            gate = r["ga"][at, :].astype(F32)
            r["hid"][at, :] = (gate / (1.0 + jnp.exp(-gate)) * r["up"][at, :].astype(F32)).astype(BF)
            return carry

        lax.fori_loop(0, tokens // 16, hide, 0)

        arrive(ro_g)
        yblock = rows_at(y * yrows, yrows)
        ro_h = [send(r["ro"].at[yblock, :], r["ro"].at[yblock, :], y_dev(dy)) for dy in Y_ORDER]
        arrive(ri_g)
        arrive(ro_h)

        def rotate(q, carry):
            at = rows_at(q * QTOK, QTOK)
            part = mm(r["ro"][at, :], r["ri"][at, :], TN)
            r["rot"][q] = (part * r["inv"][...]).astype(BF)
            return carry

        lax.fori_loop(0, NQ, rotate, 0)

        per_y = NQ // NY
        per_w = NQ // NW
        half = width_rows // 2
        for it in range(ITERS):
            basis_in, im_send = r[f"bi{it}"], r[f"im_send{it}"]
            im_y = []
            for dy in Y_ORDER + (0,):
                yy = y_at(dy)

                def image(i, carry):
                    q = yy * per_y + i
                    at = rows_at(q * RANK, RANK)
                    im_send[at, :] = mm(basis_in[at, :], r["rot"][q], NT).astype(BF)
                    return carry

                lax.fori_loop(0, per_y, image, 0)
                if dy:
                    at = rows_at(yy * per_y * RANK, per_y * RANK)
                    im_y.append(
                        send(im_send.at[at, :], r[f"im_recv{it}"].at[dy - 1], y_dev(dy))
                    )
            arrive(im_y)
            im_z = r[f"im_z{it}"]
            sum_into(im_z, im_send, y * per_y * RANK, r[f"im_recv{it}"], NY - 1, 16)

            def piece(zz):
                return (
                    rows_at(zz // 2 * RANK, RANK),
                    pl.ds(pl.multiple_of(lax.rem(zz, 2) * half, half), half),
                )

            im_zs = []
            for dz in Z_ORDER:
                rows, cols = piece(z_at(dz))
                im_zs.append(
                    send(im_z.at[rows, cols], r[f"im_zrecv{it}"].at[dz - 1], z_dev(dz))
                )
            rows, cols = piece(z)
            arrive(im_zs)
            image_cols = im_z[rows, cols].astype(F32)
            for s in range(NZ - 1):
                image_cols = image_cols + r[f"im_zrecv{it}"][s].astype(F32)
            gram = r[f"gram{it}"]
            gram[0] = mm(image_cols, image_cols, NT, HIGHEST) / D
            grams = []
            for dw in W_ORDER + (0,):
                grams.append(send(gram.at[0], gram.at[2 * dw + 1], pair_dev(dw)))
                if dw:
                    grams.append(send(gram.at[0], gram.at[2 * dw], w_dev(dw)))
            arrive(grams)
            whole = gram[0]
            for s in range(1, 2 * NW):
                whole = whole + gram[s]
            inverse = inverse_of_factor(whole)
            bo = r[f"bo{it}"]
            bo_rows = rows_at(y * per_y * RANK + z // 2 * RANK, RANK)
            bo[bo_rows, cols] = mm(inverse, image_cols, NN, HIGHEST).astype(BF)
            bo_z = [send(bo.at[bo_rows, cols], bo.at[bo_rows, cols], z_dev(dz)) for dz in Z_ORDER]
            arrive(bo_z)
            mine = rows_at(y * per_y * RANK, per_y * RANK)
            bo_y = [send(bo.at[mine, :], bo.at[mine, :], y_dev(dy)) for dy in Y_ORDER]
            arrive(bo_y)

            re_send, next_in = r[f"re_send{it}"], r[f"bi{it + 1}"]
            re_w = []
            for dw in W_ORDER + (0,):
                ww = w_at(dw)

                def transposed(i, carry):
                    q = ww * per_w + i
                    at = rows_at(q * RANK, RANK)
                    re_send[at, :] = mm(bo[at, :], r["rot"][q], NN).astype(BF)
                    return carry

                lax.fori_loop(0, per_w, transposed, 0)
                if dw:
                    at = rows_at(ww * per_w * RANK, per_w * RANK)
                    re_w.append(
                        send(re_send.at[at, :], r[f"re_recv{it}"].at[dw - 1], w_dev(dw))
                    )
            if it == ITERS - 1:
                orows = r["eo"].shape[0] // NW
                r["of_send"][...] = mm(r["eo"][...], bo[...], NT).astype(BF)
                of_w = []
                for dw in W_ORDER:
                    at = rows_at(w_at(dw) * orows, orows)
                    of_w.append(send(r["of_send"].at[at, :], r["of_recv"].at[dw - 1], w_dev(dw)))
            arrive(re_w)
            own = rows_at(w * per_w * RANK, per_w * RANK)
            sum_into(next_in.at[own, :], re_send, w * per_w * RANK, r[f"re_recv{it}"], NW - 1, 16)
            re_g = [send(next_in.at[own, :], next_in.at[own, :], w_dev(dw)) for dw in W_ORDER]
            if it == ITERS - 1:
                arrive(of_w)
                sum_into(r["of_part"], r["of_send"], w * orows, r["of_recv"], NW - 1, 16)
                owner = 2 * zlo + y // 2
                at_w = rows_at(w * orows, orows)
                of_k = count[0]
                count[0] += NW
                away = lax.rem(owner - w + NW, NW)

                def to_owner(k):
                    return pltpu.make_async_remote_copy(
                        src_ref=r["of_part"],
                        dst_ref=r["of_block"].at[at_w, :],
                        send_sem=send_sem.at[of_k],
                        recv_sem=recv_sem.at[of_k + k],
                        device_id=(zlo, y, zhi, owner),
                        device_id_type=MESH,
                    )

                @pl.when(away != 0)
                def _():
                    to_owner(away).start()

                @pl.when(away == 0)
                def _():
                    r["of_block"][at_w, :] = r["of_part"][...]

            arrive(re_g)

        basis_in = r[f"bi{ITERS}"]
        frows = ff_w // NY
        fstep = frows // 4
        if_y = []
        for dy in Y_ORDER + (0,):
            yy = y_at(dy)

            def part_if(i, carry):
                at = pl.ds(pl.multiple_of(yy * frows + i * fstep, 16), fstep)
                r["if_send"][at, :] = mm(r["ei"][at, :], basis_in[:, :ff_r], NT).astype(BF)
                return carry

            lax.fori_loop(0, 4, part_if, 0)
            if dy:
                at = rows_at(yy * frows, frows)
                if_y.append(send(r["if_send"].at[at, :], r["if_recv"].at[dy - 1], y_dev(dy)))

        orows = r["eo"].shape[0]

        @pl.when(away == 0)
        def _():
            for k in range(1, NW):
                to_owner(k).wait_recv()

        @pl.when(away != 0)
        def _():
            to_owner(away).wait_send()

        of = r["of"]
        core = lax.rem(w, 2)
        x = w // 2
        column = core == y // 2
        blk = rows_at((lax.rem(y, 2) * 2 + zhi) * orows, orows)
        of_z0 = count[0]
        count[0] += 2 * (NZ - 1)

        def along_z(dz, zh):
            return pltpu.make_async_remote_copy(
                src_ref=of.at[blk, :],
                dst_ref=of.at[blk, :],
                send_sem=send_sem.at[of_z0 + dz - 1],
                recv_sem=recv_sem.at[of_z0 + zh],
                device_id=z_dev(dz),
                device_id_type=MESH,
            )

        @pl.when(away == 0)
        def _():
            of[blk, :] = r["of_block"][...]
            for dz in Z_ORDER:
                along_z(dz, zhi).start()

        for zh in range(2):

            @pl.when(jnp.logical_and(column, z != zh * 4 + x))
            def _(zh=zh):
                along_z(1, zh).wait_recv()

        of_y0 = count[0]
        count[0] += NY
        two = rows_at(lax.rem(y, 2) * 2 * orows, 2 * orows)

        def along_y(dy, k):
            return pltpu.make_async_remote_copy(
                src_ref=of.at[two, :],
                dst_ref=of.at[two, :],
                send_sem=send_sem.at[of_y0 + dy - 1],
                recv_sem=recv_sem.at[of_y0 + k],
                device_id=y_dev(dy),
                device_id_type=MESH,
            )

        @pl.when(column)
        def _():
            for dy in Y_ORDER:
                along_y(dy, lax.rem(y, 2)).start()

        arrive(if_y)
        fsum = pl.ds(0, frows)
        sum_into(r["if_z"].at[fsum, :], r["if_send"], y * frows, r["if_recv"], NY - 1, 64)

        def share(zz, base):
            return (
                pl.ds(pl.multiple_of(base + zz // 2 * fstep, 16), fstep),
                pl.ds(pl.multiple_of(lax.rem(zz, 2) * (QR // 2), QR // 2), QR // 2),
            )

        if_zs = []
        for dz in Z_ORDER:
            rows, cols = share(z_at(dz), 0)
            if_zs.append(send(r["if_z"].at[rows, cols], r["if_zrecv"].at[dz - 1], z_dev(dz)))
        arrive(if_zs)
        rows, cols = share(z, 0)
        acc = r["if_z"][rows, cols].astype(F32)
        for s in range(NZ - 1):
            acc = acc + r["if_zrecv"][s].astype(F32)
        inf = r["inf"]
        rows, cols = share(z, y * frows)
        inf[rows, cols] = acc.astype(BF)
        if_g = [send(inf.at[rows, cols], inf.at[rows, cols], z_dev(dz)) for dz in Z_ORDER]

        for k in range(2):

            @pl.when(y != 2 * core + k)
            def _(k=k):
                along_y(1, k).wait_recv()

        loads["go"].wait()
        out_copy = pltpu.make_async_copy(of, out["of"], out_sem.at[0])
        out_copy.start()
        trows = tokens // NW

        def project_out(i, carry):
            at = rows_at(i * 128, 128)
            r["po_send"][at, :] = mm(r["go"][at, :], of[...], NN).astype(BF)
            return carry

        lax.fori_loop(0, tokens // 128, project_out, 0)
        po_w = []
        for dw in W_ORDER:
            at = rows_at(w_at(dw) * trows, trows)
            po_w.append(send(r["po_send"].at[at, :], r["po_recv"].at[dw - 1], w_dev(dw)))

        arrive(if_g)
        block = rows_at(y * frows, frows)
        if_h = [send(inf.at[block, :], inf.at[block, :], y_dev(dy)) for dy in Y_ORDER]
        arrive(if_h)
        in_copy = pltpu.make_async_copy(inf, out["inf"], out_sem.at[1])
        in_copy.start()

        def project_in(i, carry):
            at = rows_at(i * 128, 128)
            r["pi_send"][at, :] = mm(r["hid"][at, :], inf[...], NN).astype(BF)
            return carry

        lax.fori_loop(0, tokens // 128, project_in, 0)
        pi_w = []
        for dw in W_ORDER:
            at = rows_at(w_at(dw) * trows, trows)
            pi_w.append(send(r["pi_send"].at[at, :], r["pi_recv"].at[dw - 1], w_dev(dw)))
        arrive(po_w)
        arrive(pi_w)
        own = rows_at(w * trows, trows)
        proj_out = r["po_send"][own, :].astype(F32)
        proj_in = r["pi_send"][own, :].astype(F32)
        for s in range(NW - 1):
            proj_out = proj_out + r["po_recv"][s].astype(F32)
            proj_in = proj_in + r["pi_recv"][s].astype(F32)
        of_query = lax.broadcasted_iota(jnp.int32, (NQ, QR), 1) // RANK
        chosen = (of_query == lax.broadcasted_iota(jnp.int32, (NQ, QR), 0)).astype(F32)
        r["sc"][...] = mm(chosen, proj_out * proj_in, NT, HIGHEST)
        score_copy = pltpu.make_async_copy(r["sc"], out["sc"], out_sem.at[2])
        score_copy.start()

        for copy in unsent:
            copy.wait_send()

        @pl.when(away == 0)
        def _():
            for dz in Z_ORDER:
                along_z(dz, zhi).wait_send()

        @pl.when(column)
        def _():
            for dy in Y_ORDER:
                along_y(dy, lax.rem(y, 2)).wait_send()

        out_copy.wait()
        in_copy.wait()
        score_copy.wait()
        assert count[0] <= N_SEMS, count[0]

    return kernel


def per_device(
    query_out, query_in, eigen_out, eigen_in, eigvals, start, grads_out, gate_pre, up_pre
):
    args = (query_out, query_in, eigen_out, eigen_in, eigvals, start, grads_out, gate_pre, up_pre)
    shapes = {name: a.shape for name, a in zip(INPUTS, args)}
    scratch = layout_of(shapes)
    tokens = grads_out.shape[0]
    return pl.pallas_call(
        make_kernel(tuple(scratch)),
        out_shape=(
            jax.ShapeDtypeStruct((NQ, tokens // NW), F32),
            jax.ShapeDtypeStruct((eigen_out.shape[1], QR), BF),
            jax.ShapeDtypeStruct((eigen_in.shape[0], QR), BF),
        ),
        in_specs=[pl.BlockSpec(memory_space=pl.ANY)] * len(INPUTS),
        out_specs=(pl.BlockSpec(memory_space=pl.ANY),) * len(OUTPUTS),
        scratch_shapes=[pltpu.VMEM(shape, dtype) for shape, dtype in scratch.values()]
        + [
            pltpu.SemaphoreType.DMA((N_SEMS,)),
            pltpu.SemaphoreType.DMA((N_SEMS,)),
            pltpu.SemaphoreType.DMA((len(INPUTS),)),
            pltpu.SemaphoreType.DMA((len(OUTPUTS),)),
        ],
        compiler_params=pltpu.CompilerParams(
            collective_id=0, has_side_effects=True, vmem_limit_bytes=60 * 1024 * 1024
        ),
    )(*args)


def solution(mesh):
    finer = Mesh(
        mesh.devices.reshape(mesh.shape["grp"], 4, 2, mesh.shape["width"]), GRP_DP_WIDTH
    )
    placed = (
        P(None, GRP_DP),
        P(None, "width"),
        P(GRP_DP, "width"),
        P("width", GRP_DP),
        P("width", GRP_DP),
        P(GRP_DP, None),
        P(GRP_DP, "width"),
        P(GRP_DP, "width"),
        P(GRP_DP, "width"),
    )
    return jax.shard_map(
        per_device,
        mesh=finer,
        in_specs=placed,
        out_specs=(P(None, GRP_DP_WIDTH), P("width", None), P("width", None)),
        check_vma=False,
    )
```

time: 950 us -> 214 us (0.23); the launches traced: 939 us -> 213 us
  blocking collectives: 332 us -> 0 us
  waiting for transfers between devices: 304 us -> 0 us
  Pallas kernels: 0 us -> 202 us
  other arithmetic: 107 us -> 0 us
  starting transfers between devices: 60.7 us -> 0 us
  local copies, waits for them, and re-layouts: 71.4 us -> 11 us
  matrix products: 49.3 us -> 0 us
  between operations: 14.5 us -> 0.65 us
    all_to_all x10 -> x0, blocking collectives: 315 us -> none  [the longest x4 182 us: sent_and_summed(): lax.all_to_all(blocks, axis, split_axis=0, concat_axis=0, tiled=True)]
    pallas_call x0 -> x1, Pallas kernels: none -> 202 us  [per_device(): pl.pallas_call(make_kernel(tuple(scratch)), out_shape=(jax.ShapeDtypeStru...]
    all_to_all x7 -> x0, waiting for transfers between devices: 122 us -> none  [the longest x6 117 us: from_everyone(): lax.all_to_all(jnp.broadcast_to(array[None], (length, *array.shape)), axi...]
    all_gather x1 -> x0, waiting for transfers between devices: 115 us -> none  [per_device(): whole_out = lax.all_gather(block_factor, GRP_DP, axis=0, tiled=True)]
    another operation x11 -> x0, other arithmetic: 87 us -> none  [the longest x6 47.1 us: factor_inverse(): lower_factor = jnp.linalg.cholesky(gram_mat)]
    all_to_all x7 -> x0, starting transfers between devices: 60.6 us -> none  [the longest x6 41.5 us: from_everyone(): lax.all_to_all(jnp.broadcast_to(array[None], (length, *array.shape)), axi...]
    unnamed x4 -> x0, waiting for transfers between devices: 55.4 us -> none
    dot_general x15 -> x0, matrix products: 48.4 us -> none  [the longest x2 18.1 us: per_device(): jnp.einsum('qdf,dqr->fqr', rotated, basis_out, preferred_element_type=jnp...]
  transfers between devices with their start and end apart: 10 -> 0, of which waited for: 9 -> 0; matrix products, arithmetic and copies ran while one was open for 4% -> 0% of each run, Pallas kernels for 0% -> 0%
where the time goes in v1:
time: 214 us; the launch traced here: 213 us
  Pallas kernels  202 us (94%)
  local copies, waits for them, and re-layouts  11 us (5%)
    pallas_call x1, Pallas kernels, per_device(): pl.pallas_call(make_kernel(tuple(scratch)), out_shape=(jax.ShapeDtypeStru...  202 us
    unnamed x7, local copies, waits for them, and re-layouts  11 us

profile of v1, /device:TPU:1, one launch (start us, length us, event | category | flops | bytes accessed | tf_op | source)
XLA Modules:
  0.0 213.5 jit_solution(10904145116224494396)
XLA Ops:
  0.6 0.0 copy-start
  0.6 3.9 %copy.12.refs_3_ = bf16[1792,448]{1,0:T(8,128)(2,1)} copy(bf16[1792,448]{0,1:T(8,128)(2,1)} %param.12) | data formatting | bytes 3211264 | tf_op args[3]
  4.5 0.0 copy-done
  4.5 1.8 copy.13.refs_4_
  6.4 201.8 %shard_map.112 = (f32[16,64]{1,0:T(8,128)}, bf16[1024,256]{1,0:T(8,128)(2,1)}, bf16[1792,256]{1,0:T(8,128)(2,1)}) custom-call(bf16[512,256]{1,0:T(8,128)(2,1)} %refs_0_.1, bf16[512,1792]{1,0:T(8,128)(2,1)} %refs_1_.1, bf16[256,1024]{1,0:T(8,128)(2,1)} %refs_2_.1, bf16[1792,448]{1,0:T(8,128)(2,1)} %copy.12.refs_3_, f32[1024,448]{1,0:T(8,128)} %copy.13.refs_4_, ...), custom_call_target="tpu_custom_call" | custom-call | tf_op jit(solution)/shard_map/pallas_call | solution.py:602
  208.2 1.3 copy.17
  209.5 1.9 copy.18
  211.3 2.2 %copy.19 = bf16[1792,256]{1,0:T(8,128)(2,1)} copy(bf16[1792,256]{1,0:T(8,128)(2,1)} %get-tuple-element.8) | data formatting | bytes 1835008
Async XLA Ops:
  0.6 3.9 %copy-start = (f32[1024,448]{0,1:T(8,128)S(1)}, f32[1024,448]{0,1:T(8,128)}, u32[]{:S(2)}) copy-start(f32[1024,448]{0,1:T(8,128)} %param.13) | copy-start | bytes 5505028
